TPU v7x, 512 devices: a whole 4x4x16 slice. The times are simulated.
512 devices in a mesh: dp: 8 (over y, z_hi), rows: 64 (over z_lo, x, core).
Axes of the slice: x: 4, y: 4, z: 16 (z_hi: 2, z_lo: 8; z = z_hi * 8 + z_lo), core: 2. Of those that a mesh axis runs over, the one named last changes fastest.
Arguments:
- features: bfloat16 [8, 256, 256, 128], P('dp', 'rows'), may hold values from -6 to 6
- conv_weight: bfloat16 [3, 3, 128, 128], replicated, may hold values from -0.1875 to 0.1875
- out_weight: bfloat16 [128, 3], replicated, may hold values from -0.5 to 0.5
- targets: float32 [8, 256, 256, 3], P('dp', 'rows'), may hold values from -4 to 4
- disc_weight: float32 [3, 3, 3, 64], replicated, may hold values from -1.25 to 1.25
- disc_head: float32 [64], replicated, may hold values from -0.75 to 0.75
- lpips_weight: float32 [3, 3, 3, 64], replicated, may hold values from -1.25 to 1.25
- lpips_lin: float32 [64], replicated, may hold values from 0.1 to 1
Outputs:
- recon: float32 [8, 256, 256, 3], P('dp', 'rows')
- grad_features: bfloat16 [8, 256, 256, 128], P('dp', 'rows')
- grad_conv: float32 [3, 3, 128, 128], P(None, None, None, 'dp')
- grad_out: float32 [128, 3], P('dp')
All inputs are finite; a program needn't handle non-finite values.
Results may differ from a plain program's by a relative error of at most 0.01.
Values may be sent and summed in bfloat16 or wider, within the bound.
No kernel may reach another device: no remote copies, remote signals or barrier semaphores. Data moves between devices by JAX's collectives and lax.ppermute only.
A program may use at most 64 MiB of HBM per device.

v0:
```python
import jax
import jax.numpy as jnp
from jax import lax
from jax.experimental import pallas as pl
from jax.experimental.pallas import tpu as pltpu
from jax.sharding import Mesh, PartitionSpec as P

ADV_SCALE = 0.5
CHARB_EPS = 0.01
NORM_EPS = 1e-06
GELU_K = 0.7978845608028654
GELU_C = 0.044715

ROWS_LOC = 4
COLS = 256
TILE = ROWS_LOC * COLS
CH = 128
TILES = 64
HEIGHT = ROWS_LOC * TILES
HALO = 3
SLAB = HALO * COLS
N_PRE = 8
N_LOSS = 6
N_GRAD = 4
PITCH = COLS + 8
K_BAND = 256
BLOCK = 20
PADDED = 24
VMEM = pltpu.VMEM


def select_ahead(r):
    lane = lax.broadcasted_iota(jnp.int32, (32, K_BAND), 1)
    b, j, c = lane // (N_PRE * 8), (lane // 8) % N_PRE, lane % 8
    return chosen(lax.broadcasted_iota(jnp.int32, (32, K_BAND), 0), j - r, b, c)


def select_back(r):
    dims = (3 * N_GRAD * 8, 32)
    line = lax.broadcasted_iota(jnp.int32, dims, 0)
    b, q, c = line // (N_GRAD * 8), (line // 8) % N_GRAD, line % 8
    return chosen(lax.broadcasted_iota(jnp.int32, dims, 1), q + 2 - r, b, c)


def chosen(tap, a, b, c):
    real = jnp.logical_and(jnp.logical_and(a >= 0, a < 3), jnp.logical_and(b < 3, c < 3))
    hit = jnp.logical_and(real, tap == 9 * a + 3 * b + c)
    return jnp.where(hit, 1.0, 0.0).astype(jnp.bfloat16)


def dot(a, b, ca, cb):
    return lax.dot_general(a, b, (((ca,), (cb,)), ((), ())), preferred_element_type=jnp.float32)


def sigmoid(x):
    return 1.0 / (1.0 + jnp.exp(-jnp.maximum(x, -87.0)))


def shifted(x, by):
    lane = lax.broadcasted_iota(jnp.int32, x.shape, 1)
    if by == 1:
        return jnp.where(lane == 0, 0.0, pltpu.roll(x, 1, 1))
    return jnp.where(lane == COLS - 1, 0.0, pltpu.roll(x, COLS - 1, 1))


def pack_kernel(tile_ref, own_ref, truth_ref, near_ref, far_ref, truth_vmem, sems):
    first = lax.rem(tile_ref[0], 2) == 0
    fetch = pltpu.make_async_copy(truth_ref, truth_vmem, sems.at[2])
    fetch.start()

    def slabs(top_ref, bottom_ref):
        top = pltpu.make_async_copy(
            own_ref.at[pl.ds(0, SLAB)], top_ref.at[pl.ds(0, SLAB)], sems.at[0]
        )
        bottom = pltpu.make_async_copy(
            own_ref.at[pl.ds(COLS, SLAB)], bottom_ref.at[pl.ds(0, SLAB)], sems.at[1]
        )
        top.start()
        bottom.start()
        fetch.wait()
        rows = [
            truth_vmem[c, :, h * CH : (h + 1) * CH] for c in range(3) for h in range(COLS // CH)
        ] + [jnp.zeros((8, CH), jnp.float32)]
        high = jnp.concatenate(rows, axis=0).astype(jnp.bfloat16)
        near_ref[pl.ds(SLAB, 32), :] = high
        far_ref[pl.ds(SLAB, 32), :] = high
        top.wait()
        bottom.wait()

    @pl.when(first)
    def _():
        slabs(far_ref, near_ref)

    @pl.when(jnp.logical_not(first))
    def _():
        slabs(near_ref, far_ref)


def prep_kernel(
    disc_ref, lpips_ref, head_ref, lin_ref, out_w_ref, conv_ref,
    band_ref, band_t_ref, heads_ref, wide_ref, two_ref, w27_ref,
):
    w27_ref[...] = jnp.zeros_like(w27_ref)
    for a in range(3):
        for b in range(3):
            pair = jnp.concatenate([disc_ref[a, b], lpips_ref[a, b]], axis=1)
            w27_ref[pl.ds((a * 3 + b) * 3, 3), :] = pair
    w27 = w27_ref[...].astype(jnp.bfloat16)
    for r in range(N_LOSS):
        band = dot(w27, select_ahead(r), 0, 0)
        band_ref[r * CH : r * CH + CH // 2, :] = (0.5 * band[: CH // 2]).astype(jnp.bfloat16)
        band_ref[r * CH + CH // 2 : (r + 1) * CH, :] = band[CH // 2 :].astype(jnp.bfloat16)
        back = dot(select_back(r), w27, 1, 0)
        band_t_ref[:, r * CH : (r + 1) * CH] = back.astype(jnp.bfloat16)
    line = jnp.concatenate([-0.4 * ADV_SCALE * head_ref[...], 2.0 * lin_ref[...]], axis=1)
    heads_ref[...] = jnp.broadcast_to(line, (CH, CH)).T
    wide_ref[...] = jnp.zeros_like(wide_ref)
    wide_ref[0:3, :] = out_w_ref[...].astype(jnp.float32)
    zero = jnp.zeros((CH, CH), jnp.bfloat16)
    for b in range(3):
        for k in range(4):
            two_ref[b, k * CH : (k + 1) * CH, :CH] = conv_ref[k, b] if k < 3 else zero
            two_ref[b, k * CH : (k + 1) * CH, CH:] = conv_ref[k - 1, b] if k else zero


def main_kernel(
    tile_ref, far_ref, own_ref, truth_ref, near_ref, two_ref, out_w_ref,
    band_ref, band_t_ref, heads_ref,
    recon_ref, grad_pre_ref, near_edge_ref, far_edge_ref, piece_ref,
    y0, y1, y2, slope, hidden, truth, dall, packed, up_ref, down_ref,
):
    bf16, f32 = jnp.bfloat16, jnp.float32

    first = lax.rem(tile_ref[0], 2) == 0

    @pl.when(first)
    def _():
        up_ref[...] = far_ref[...]
        down_ref[...] = near_ref[...]

    @pl.when(jnp.logical_not(first))
    def _():
        up_ref[...] = near_ref[...]
        down_ref[...] = far_ref[...]

    first_row = tile_ref[0] * ROWS_LOC

    def valid(row):
        inside = jnp.logical_and(first_row + row >= 0, first_row + row < HEIGHT)
        return jnp.where(inside, 1.0, 0.0).astype(f32)

    def feats(j):
        if j < HALO:
            return up_ref[pl.ds(j * COLS, COLS), :]
        if j < HALO + ROWS_LOC:
            return own_ref[pl.ds((j - HALO) * COLS, COLS), :]
        return down_ref[pl.ds((j - HALO - ROWS_LOC) * COLS, COLS), :]

    for buf in (y0, y2):
        for j in range(N_PRE + 1):
            buf[pl.ds(j * PITCH, 8), :] = jnp.zeros((8, CH), f32)
    out_w = out_w_ref[...]
    out_w16 = out_w.astype(bf16)
    image = []
    for j in range(0, N_PRE, 2):
        lhs = jnp.concatenate([feats(j + k) for k in range(4)], axis=1)
        for b, buf in enumerate((y0, y1, y2)):
            prod = dot(lhs, two_ref[b], 1, 0)
            buf[pl.ds(j * PITCH + 8, COLS), :] = prod[:, :CH]
            buf[pl.ds((j + 1) * PITCH + 8, COLS), :] = prod[:, CH:]
    for j in range(N_PRE):
        at = j * PITCH + 8
        pre = y0[pl.ds(at - 1, COLS), :] + y1[pl.ds(at, COLS), :] + y2[pl.ds(at + 1, COLS), :]
        sig = sigmoid(pre)
        act = (pre * sig).astype(bf16)
        seen = dot(out_w16, act, 1, 1)
        if 2 <= j < 2 + ROWS_LOC:
            slope[j - 2] = sig * (1.0 + pre * (1.0 - sig))
            hidden[j - 2] = act
        else:
            seen = seen * valid(j - 2)
        image.append(seen)
    for j in range(ROWS_LOC):
        for c in range(3):
            recon_ref[c, j : j + 1, :] = image[j + 2][c : c + 1, :]
    image = jnp.concatenate(image, axis=0)

    truth[...] = jnp.zeros_like(truth)
    for k, ref in ((-1, up_ref), (1, down_ref)):
        rows = ref[pl.ds(SLAB, 32), :].astype(f32)
        for y in range(2):
            row, j = (y + 2, y) if k < 0 else (y, y + 6)
            for c in range(3):
                for h in range(COLS // CH):
                    at = (c * 2 + h) * ROWS_LOC + row
                    truth[j * 8 + c : j * 8 + c + 1, h * CH : (h + 1) * CH] = rows[at : at + 1]
    for y in range(ROWS_LOC):
        for c in range(3):
            at = (y + 2) * 8 + c
            truth[at : at + 1, :] = truth_ref[c, y : y + 1, :]
    true_image = truth[...]

    def taps(x):
        pad = jnp.zeros((K_BAND - 3 * N_PRE * 8, COLS), f32)
        return jnp.concatenate([shifted(x, 1), x, shifted(x, -1), pad], axis=0).astype(bf16)

    taps_a, taps_b = taps(image), taps(true_image)
    half = CH // 2

    def gelu(x):
        sq = x * x
        th = jnp.tanh(x * (GELU_K + (GELU_K * GELU_C) * sq))
        rise = 1.0 + th
        return x * rise, rise, th, sq

    def norm(twice):
        mean = jnp.sum(twice * twice, axis=0, keepdims=True) * (1.0 / half)
        return lax.rsqrt(mean + 4.0 * NORM_EPS)

    for r in range(N_LOSS):
        inside = 1 <= r < 1 + ROWS_LOC
        ok = 1.0 if inside else valid(r - 1)
        both = dot(band_ref[r * CH : (r + 1) * CH, :], taps_a, 1, 0)
        other = dot(band_ref[r * CH + half : (r + 1) * CH, :], taps_b, 1, 0)
        for side in range(2):
            cols = slice(side * CH, (side + 1) * CH)
            g, a, t = both[:half, cols], both[half:, cols], other[:, cols]
            head = heads_ref[:half, :] if inside else heads_ref[:half, :] * ok
            d_disc = head * (1.5 + jnp.tanh(g))
            fa, rise, th, sq = gelu(a)
            fb = gelu(t)[0]
            inv_a, inv_b = norm(fa), norm(fb)
            na = fa * inv_a
            up = heads_ref[half:, :] * (na - fb * inv_b)
            mean = jnp.sum(up * na, axis=0, keepdims=True) * (1.0 / half)
            d_feat = (inv_a * ok) * (up - na * mean)
            slant = rise + fa * (1.0 - th) * (GELU_K + (3.0 * GELU_K * GELU_C) * sq)
            dall[r * CH : r * CH + half, cols] = d_disc.astype(bf16)
            dall[r * CH + half : (r + 1) * CH, cols] = (d_feat * slant).astype(bf16)

    back = dot(band_t_ref[...], dall[...], 1, 0)
    n = N_GRAD * 8
    diff = (image - true_image)[16 : 16 + n]
    grad_image = (
        shifted(back[:n], -1) + back[n : 2 * n] + shifted(back[2 * n :], 1)
        + diff * lax.rsqrt(diff * diff + CHARB_EPS)
    )
    out_w2 = jnp.concatenate([out_w, out_w], axis=0).astype(bf16)
    grad_out = jnp.zeros((16, CH), f32)
    for q in range(N_GRAD):
        g = grad_image[q * 8 : (q + 1) * 8]
        high = g.astype(bf16).astype(f32)
        pair = jnp.concatenate([high, g - high], axis=0)
        grad_pre = dot(pair.T.astype(bf16), out_w2, 1, 0) * slope[q]
        grad_pre_ref[q] = grad_pre.astype(bf16)
        y0[pl.ds(q * PITCH + 8, COLS), :] = grad_pre
        grad_out = grad_out + dot(pair.astype(bf16), hidden[q], 1, 0)
    grad_out = grad_out[:8] + grad_out[8:]

    edge = jnp.where(first, 0, ROWS_LOC - 1)
    far_edge_ref[...] = grad_pre_ref[edge]
    near_edge_ref[...] = grad_pre_ref[ROWS_LOC - 1 - edge]

    lhs, rhs = [], []
    for y in range(ROWS_LOC):
        at = y * PITCH + 8
        lhs.append(
            jnp.concatenate([y0[pl.ds(at + 1 - b, COLS), :] for b in range(3)], axis=1).astype(bf16)
        )
        rhs.append(jnp.concatenate([feats(2 + y + a) for a in range(3)], axis=1))
    lhs, rhs = jnp.concatenate(lhs, axis=0), jnp.concatenate(rhs, axis=0)
    for k in range(64):
        packed[pl.ds(k * BLOCK + 18, 2), :] = jnp.zeros((2, CH), f32)
    for b in range(3):
        grad = dot(lhs[:, b * CH : (b + 1) * CH], rhs, 0, 0)
        for a in range(3):
            tap = a * 3 + b
            for d in range(8):
                block = grad[d * 16 : (d + 1) * 16, a * CH : (a + 1) * CH]
                start = tap * 16
                while start < tap * 16 + 16:
                    part, inner = divmod(start, 18)
                    count = min(18 - inner, tap * 16 + 16 - start)
                    at = ((d // 2) * 8 + part) * 2 * BLOCK + (d % 2) * BLOCK + inner
                    packed[pl.ds(at, count), :] = block[start - tap * 16 : start - tap * 16 + count]
                    start += count
    for d in range(8):
        for c in range(3):
            line = grad_out[c : c + 1]
            if d:
                line = pltpu.roll(line, CH - 16 * d, 1)
            packed[pl.ds(((d // 2) * 8 + c) * 2 * BLOCK + (d % 2) * BLOCK + 18, 1), :] = line
    piece_ref[...] = packed[...].astype(bf16)


def back_kernel(
    tile_ref, grad_ref, far_ref, near_ref, conv_ref, recon_ref,
    out_ref, recon_out_ref, z0, z1, z2, wide_ref,
):
    bf16, f32 = jnp.bfloat16, jnp.float32
    recon_out_ref[...] = recon_ref[...]
    first = lax.rem(tile_ref[0], 2) == 0
    wide_ref[1 : 1 + ROWS_LOC] = grad_ref[...]

    @pl.when(first)
    def _():
        wide_ref[0] = far_ref[...]
        wide_ref[ROWS_LOC + 1] = near_ref[...]

    @pl.when(jnp.logical_not(first))
    def _():
        wide_ref[0] = near_ref[...]
        wide_ref[ROWS_LOC + 1] = far_ref[...]

    for buf in (z0, z2):
        for y in range(ROWS_LOC + 1):
            buf[pl.ds(y * PITCH, 8), :] = jnp.zeros((8, CH), f32)
    weights = jnp.concatenate(
        [jnp.concatenate([conv_ref[a, b] for a in range(3)], axis=1) for b in range(3)], axis=0
    )
    for y in range(ROWS_LOC):
        lhs = jnp.concatenate([wide_ref[y + 2 - a] for a in range(3)], axis=1)
        prod = dot(lhs, weights, 1, 1)
        for b, buf in enumerate((z0, z1, z2)):
            buf[pl.ds(y * PITCH + 8, COLS), :] = prod[:, b * CH : (b + 1) * CH]
    for y in range(ROWS_LOC):
        at = y * PITCH + 8
        total = z0[pl.ds(at + 1, COLS), :] + z1[pl.ds(at, COLS), :] + z2[pl.ds(at - 1, COLS), :]
        out_ref[y] = total.astype(bf16)


def first_sum_kernel(in_ref, out_ref):
    total = in_ref[0].astype(jnp.float32)
    for k in range(1, in_ref.shape[0]):
        total = total + in_ref[k].astype(jnp.float32)
    pad = jnp.zeros((PADDED - BLOCK, CH), jnp.float32)
    for half in range(2):
        part = jnp.concatenate([total[half * BLOCK : (half + 1) * BLOCK], pad], axis=0)
        for k in range(8):
            out_ref[half * 8 + k] = part.astype(jnp.bfloat16)


def second_sum_kernel(in_ref, out_ref):
    total = in_ref[0].astype(jnp.float32)
    for k in range(1, in_ref.shape[0]):
        total = total + in_ref[k].astype(jnp.float32)
    for k in range(8):
        out_ref[k] = total


def last_kernel(in_ref, conv_ref, out_ref):
    for k in range(8):
        conv_ref[pl.ds(k * 18, 18), :] = in_ref[k, 0:18, :]
    for c in range(3):
        out_ref[c : c + 1, :] = in_ref[c, 18:19, :16]


def call(kernel, out_shape, scratch=(), smem=0, whole=0, n_in=1, flops=0, vmem=4):
    specs = [pl.BlockSpec(memory_space=pltpu.SMEM)] * smem
    specs += [pl.BlockSpec(memory_space=pltpu.HBM)] * whole
    specs += [pl.BlockSpec(memory_space=VMEM)] * (n_in - smem - whole)
    many = isinstance(out_shape, tuple)
    return pl.pallas_call(
        kernel,
        out_shape=out_shape,
        in_specs=specs,
        out_specs=tuple(pl.BlockSpec(memory_space=VMEM) for _ in out_shape)
        if many
        else pl.BlockSpec(memory_space=VMEM),
        scratch_shapes=list(scratch),
        cost_estimate=pl.CostEstimate(flops=flops, bytes_accessed=1 << 20, transcendentals=0),
        compiler_params=pltpu.CompilerParams(vmem_limit_bytes=vmem << 20),
    )


def shape(*dims, dtype=jnp.float32):
    return jax.ShapeDtypeStruct(dims, dtype)


def pack(tile, features, targets):
    out = shape(SLAB + 32, CH, dtype=jnp.bfloat16)
    return call(
        pack_kernel,
        (out, out),
        scratch=[VMEM((3, ROWS_LOC, COLS), jnp.float32), pltpu.SemaphoreType.DMA((3,))],
        smem=1,
        n_in=3,
        whole=2,
    )(
        tile,
        pltpu.with_memory_space_constraint(features, pltpu.HBM),
        pltpu.with_memory_space_constraint(targets, pltpu.HBM),
    )


def prepare(conv_weight, disc_weight, disc_head, lpips_weight, lpips_lin, out_weight):
    bf16 = jnp.bfloat16
    return call(
        prep_kernel,
        (
            shape(N_LOSS * CH, K_BAND, dtype=bf16),
            shape(3 * N_GRAD * 8, N_LOSS * CH, dtype=bf16),
            shape(CH, CH),
            shape(8, CH),
            shape(3, 4 * CH, 2 * CH, dtype=bf16),
        ),
        scratch=[VMEM((32, CH), jnp.float32)],
        n_in=6,
        flops=1 << 28,
    )(
        disc_weight, lpips_weight, disc_head.reshape(1, -1), lpips_lin.reshape(1, -1),
        out_weight.T, conv_weight,
    )


def tile_step(tile, far, own, truth, near, band, band_t, heads, out_w, two):
    f32, bf16 = jnp.float32, jnp.bfloat16
    rows = N_PRE * PITCH + 8
    return call(
        main_kernel,
        (
            shape(3, ROWS_LOC, COLS),
            shape(ROWS_LOC, COLS, CH, dtype=bf16),
            shape(COLS, CH, dtype=bf16),
            shape(COLS, CH, dtype=bf16),
            shape(32 * 2 * BLOCK, CH, dtype=bf16),
        ),
        scratch=[
            VMEM((rows, CH), f32),
            VMEM((rows, CH), f32),
            VMEM((rows, CH), f32),
            VMEM((N_GRAD, COLS, CH), f32),
            VMEM((ROWS_LOC, COLS, CH), bf16),
            VMEM((N_PRE * 8, COLS), f32),
            VMEM((N_LOSS * CH, COLS), bf16),
            VMEM((32 * 2 * BLOCK, CH), f32),
            VMEM((SLAB + 32, CH), bf16),
            VMEM((SLAB + 32, CH), bf16),
        ],
        smem=1,
        n_in=10,
        flops=1 << 31,
        vmem=20,
    )(tile, far, own, truth, near, two, out_w, band, band_t, heads)


def back_step(tile, grad_pre, far, near, conv_weight, recon):
    rows = ROWS_LOC * PITCH + 8
    return call(
        back_kernel,
        (shape(ROWS_LOC, COLS, CH, dtype=jnp.bfloat16), shape(3, ROWS_LOC, COLS)),
        scratch=[VMEM((rows, CH), jnp.float32)] * 3
        + [VMEM((ROWS_LOC + 2, COLS, CH), jnp.bfloat16)],
        smem=1,
        n_in=6,
        flops=1 << 30,
        vmem=8,
    )(tile, grad_pre, far, near, conv_weight, recon)


def swap(array, axes):
    return lax.all_to_all(array, axes, split_axis=0, concat_axis=0, tiled=True)


def swaps(firsts):
    return [pair for i in firsts for pair in ((i, i + 1), (i + 1, i))]


ROWS = ("zl", "x", "core")


def body(
    features, conv_weight, out_weight, targets, disc_weight, disc_head, lpips_weight, lpips_lin
):
    tile = lax.axis_index(ROWS).astype(jnp.int32).reshape(1)
    own, truth = features[0].reshape(TILE, CH), jnp.transpose(targets[0], (2, 0, 1))
    on_chip, off_chip = swaps(range(0, TILES, 2)), swaps(range(1, TILES - 1, 2))
    near, far = pack(tile, own, truth)
    near, far = lax.ppermute(near, ROWS, on_chip), lax.ppermute(far, ROWS, off_chip)
    tables = prepare(
        conv_weight, disc_weight, disc_head, lpips_weight, lpips_lin, out_weight
    )
    recon, grad_pre, near, far, pieces = tile_step(tile, far, own, truth, near, *tables)
    pieces = swap(pieces.reshape(32, 2 * BLOCK, CH), ("y", "x", "core"))
    pieces = call(first_sum_kernel, shape(16, PADDED, CH, dtype=jnp.bfloat16))(pieces)
    pieces, near, far = lax.optimization_barrier((pieces, near, far))
    pieces = swap(pieces, ("zh", "zl"))
    near, far = lax.ppermute(near, ROWS, on_chip), lax.ppermute(far, ROWS, off_chip)
    grad_features, recon = back_step(tile, grad_pre, far, near, conv_weight, recon)
    pieces, grad_features, recon = lax.optimization_barrier((pieces, grad_features, recon))
    pieces = call(second_sum_kernel, shape(8, PADDED, CH))(pieces)
    pieces = swap(pieces, ("x", "core"))
    grad_conv, grad_out = call(last_kernel, (shape(144, CH), shape(3, 16)))(pieces)
    return (
        jnp.transpose(recon, (1, 2, 0))[None],
        grad_features[None],
        jnp.transpose(grad_conv.reshape(3, 3, 16, CH), (0, 1, 3, 2)),
        grad_out.T,
    )


def solution(mesh):
    fine = Mesh(mesh.devices.reshape(4, 2, 8, 4, 2), ("y", "zh", "zl", "x", "core"))
    dp = ("y", "zh")
    in_specs = (
        P(dp, ROWS, None, None), P(), P(), P(dp, ROWS, None, None), P(), P(), P(), P(),
    )
    out_specs = (
        P(dp, ROWS, None, None), P(dp, ROWS, None, None), P(None, None, None, dp), P(dp, None),
    )
    return jax.shard_map(body, mesh=fine, in_specs=in_specs, out_specs=out_specs, check_vma=False)
```

profile of v0, /device:TPU:1, one launch (start us, length us, event | category | flops | bytes accessed | tf_op | source)
XLA Modules:
  0.0 69.5 jit_solution(8061853256935722311)
XLA Ops:
  0.6 0.0 copy-start.2
  0.6 0.0 copy-start.3
  0.7 1.1 %shard_map.111 = (bf16[800,128]{1,0:T(8,128)(2,1)S(1)}, bf16[800,128]{1,0:T(8,128)(2,1)S(1)}) custom-call(s32[1]{0:T(128)} %bitcast.tile_ref, bf16[1024,128]{1,0:T(8,128)(2,1)} %bitcast.18, f32[3,4,256]{2,1,0:T(4,128)} %bitcast.20), custom_call_target="tpu_custom_call" | custom-call | bytes 1048576 | tf_op jit(solution)/shard_map/pallas_call | solution.py:382
  1.8 4.5 %collective-permute-start = (bf16[800,128]{1,0:T(8,128)(2,1)S(1)}, bf16[800,128]{1,0:T(8,128)(2,1)S(1)}, u32[]{:S(2)}, u32[]{:S(2)}) collective-permute-start(bf16[800,128]{1,0:T(8,128)(2,1)S(1)} %get-tuple-element.26), channel_id=1, source_target_pairs={{1,2},{2,1},{3,4},{4,3},{5,6},{6,5},{7,8},{8,7},{9,10},{10,9},{11,... | collective-permute-start | bytes 614408 | tf_op jit(solution)/shard_map/ppermute | solution.py:479
  6.3 4.9 %collective-permute-start.1 = (bf16[800,128]{1,0:T(8,128)(2,1)S(1)}, bf16[800,128]{1,0:T(8,128)(2,1)S(1)}, u32[]{:S(2)}, u32[]{:S(2)}) collective-permute-start(bf16[800,128]{1,0:T(8,128)(2,1)S(1)} %get-tuple-element.27), channel_id=1, source_target_pairs={{0,1},{1,0},{2,3},{3,2},{4,5},{5,4},{6,7},{7,6},{8,9},{9,8},{10,11... | collective-permute-start | bytes 614408 | tf_op jit(solution)/shard_map/ppermute | solution.py:479
  11.2 0.0 copy-start.7
  11.2 0.0 copy-start.5
  11.2 0.0 copy-start.6
  11.2 0.0 copy-done.2
  11.3 0.0 copy-done.3
  11.3 0.6 copy-done.7
  11.9 0.0 copy-done.5
  11.9 0.0 copy-done.6
  11.9 0.0 copy-start.4
  11.9 0.7 %copy-done.4 = f32[3,3,3,64]{3,2,1,0:T(4,128)S(1)} copy-done((f32[3,3,3,64]{3,2,1,0:T(4,128)S(1)}, f32[3,3,3,64]{3,2,1,0:T(4,128)}, u32[]{:S(2)}) %copy-start.4) | copy-done | bytes 6936
  12.6 0.0 copy-start
  12.6 0.0 copy-start.1
  12.6 0.5 shard_map.112
  13.1 0.0 collective-permute-done.far_ref
  13.1 0.0 collective-permute-done.1.near_ref
  13.1 0.5 copy-done
  13.6 0.0 copy-done.1
  13.6 3.4 %shard_map.113 = (f32[3,4,256]{2,1,0:T(4,128)S(1)}, bf16[4,256,128]{2,1,0:T(8,128)(2,1)S(1)}, bf16[256,128]{1,0:T(8,128)(2,1)S(1)}, bf16[256,128]{1,0:T(8,128)(2,1)S(1)}, bf16[1280,128]{1,0:T(8,128)(2,1)S(1)}) custom-call(s32[1]{0:T(128)} %bitcast.tile_ref, bf16[800,128]{1,0:T(8,128)(2,1)S(1)} %collective-permute-done.far_ref, ...), custom_call_target="tpu_custom_call" | custom-call | flops 2147483648 | bytes 1048576 | tf_op jit(solution)/shard_map/pallas_call | solution.py:419
  17.0 14.5 %all_to_all.15.in_ref = bf16[32,40,128]{2,1,0:T(8,128)(2,1)S(1)} all-to-all(bf16[32,40,128]{2,1,0:T(8,128)(2,1)S(1)} %bitcast.17), channel_id=1, replica_groups=mesh['y'=4,'zh'=2,'zl'=8,'x'=4,'core'=2] {'y','x','core'}, dimensions={0} | all-to-all | bytes 655360 | tf_op jit(solution)/shard_map/all_to_all | solution.py:462
  31.4 0.7 %shard_map.114 = bf16[16,24,128]{2,1,0:T(8,128)(2,1)} custom-call(bf16[32,40,128]{2,1,0:T(8,128)(2,1)S(1)} %all_to_all.15.in_ref), custom_call_target="tpu_custom_call" | custom-call | bytes 1048576 | tf_op jit(solution)/shard_map/pallas_call | solution.py:485
  32.1 14.9 %all-to-all-start.1 = ((bf16[16,24,128]{2,1,0:T(8,128)(2,1)}), bf16[16,24,128]{2,1,0:T(8,128)(2,1)S(1)}, u32[]{:S(2)}, u32[]{:S(2)}) async-start(bf16[16,24,128]{2,1,0:T(8,128)(2,1)} %shard_map.114), calls=%async_computation.1 | async-start | bytes 196608 | tf_op jit(solution)/shard_map/all_to_all | solution.py:462
  47.0 2.6 %collective-permute-start.2 = (bf16[256,128]{1,0:T(8,128)(2,1)S(1)}, bf16[256,128]{1,0:T(8,128)(2,1)S(1)}, u32[]{:S(2)}, u32[]{:S(2)}) collective-permute-start(bf16[256,128]{1,0:T(8,128)(2,1)S(1)} %get-tuple-element.38), channel_id=1, source_target_pairs={{1,2},{2,1},{3,4},{4,3},{5,6},{6,5},{7,8},{8,7},{9,10},{10,9},{11,... | collective-permute-start | bytes 196616 | tf_op jit(solution)/shard_map/ppermute | solution.py:488
  49.6 1.9 %collective-permute-start.3 = (bf16[256,128]{1,0:T(8,128)(2,1)S(1)}, bf16[256,128]{1,0:T(8,128)(2,1)S(1)}, u32[]{:S(2)}, u32[]{:S(2)}) collective-permute-start(bf16[256,128]{1,0:T(8,128)(2,1)S(1)} %get-tuple-element.39), channel_id=1, source_target_pairs={{0,1},{1,0},{2,3},{3,2},{4,5},{5,4},{6,7},{7,6},{8,9},{9,8},{10,11... | collective-permute-start | bytes 196616 | tf_op jit(solution)/shard_map/ppermute | solution.py:488
  51.6 1.4 %collective-permute-done.2.far_ref = bf16[256,128]{1,0:T(8,128)(2,1)S(1)} collective-permute-done((bf16[256,128]{1,0:T(8,128)(2,1)S(1)}, bf16[256,128]{1,0:T(8,128)(2,1)S(1)}, u32[]{:S(2)}, u32[]{:S(2)}) %collective-permute-start.2) | collective-permute-done | bytes 65568 | tf_op jit(solution)/shard_map/ppermute | solution.py:488
  52.9 0.0 collective-permute-done.3.near_ref
  52.9 1.5 %shard_map.115 = (bf16[4,256,128]{2,1,0:T(8,128)(2,1)}, f32[3,4,256]{2,1,0:T(4,128)}) custom-call(s32[1]{0:T(128)} %bitcast.tile_ref, bf16[4,256,128]{2,1,0:T(8,128)(2,1)S(1)} %get-tuple-element.37.grad_ref, bf16[256,128]{1,0:T(8,128)(2,1)S(1)} %collective-permute-done.2.far_ref, bf16[256,128]{1,0:T(8,128)(2,1)S(1)} %collective-permute-done.3.near_ref, ...), custom_call_target="tpu_custom_call" | custom-call | flops 1073741824 | bytes 1048576 | tf_op jit(solution)/shard_map/pallas_call | solution.py:449
  54.4 4.5 %all-to-all-done.1.in_ref = bf16[16,24,128]{2,1,0:T(8,128)(2,1)S(1)} async-done(((bf16[16,24,128]{2,1,0:T(8,128)(2,1)}), bf16[16,24,128]{2,1,0:T(8,128)(2,1)S(1)}, u32[]{:S(2)}, u32[]{:S(2)}) %all-to-all-start.1) | async-done | bytes 98336 | tf_op jit(solution)/shard_map/all_to_all | solution.py:462
  59.0 9.9 %all_to_all.16.in_ref = f32[8,24,128]{2,1,0:T(8,128)S(1)} all-to-all(f32[8,24,128]{2,1,0:T(8,128)S(1)} %shard_map.116), channel_id=1, replica_groups=mesh['y'=4,'zh'=2,'zl'=8,'x'=4,'core'=2] {'x','core'}, dimensions={0} | all-to-all | bytes 196608 | tf_op jit(solution)/shard_map/all_to_all | solution.py:462
  68.9 0.6 shard_map.117
  (1 shorter events, 0.0 us)
Async XLA Ops:
  0.6 10.6 %copy-start.2 = (bf16[3,3,128,128]{3,2,1,0:T(8,128)(2,1)S(1)}, bf16[3,3,128,128]{3,2,1,0:T(8,128)(2,1)}, u32[]{:S(2)}) copy-start(bf16[3,3,128,128]{3,2,1,0:T(8,128)(2,1)} %conv_ref.3) | copy-start | bytes 884740
  0.6 10.6 %copy-start.3 = (f32[3,3,3,64]{3,2,1,0:T(4,128)S(1)}, f32[3,3,3,64]{3,2,1,0:T(4,128)}, u32[]{:S(2)}) copy-start(f32[3,3,3,64]{3,2,1,0:T(4,128)} %disc_ref.1) | copy-start | bytes 20740
  1.8 11.3 %collective-permute-start = (bf16[800,128]{1,0:T(8,128)(2,1)S(1)}, bf16[800,128]{1,0:T(8,128)(2,1)S(1)}, u32[]{:S(2)}, u32[]{:S(2)}) collective-permute-start(bf16[800,128]{1,0:T(8,128)(2,1)S(1)} %get-tuple-element.26), channel_id=1, source_target_pairs={{1,2},{2,1},{3,4},{4,3},{5,6},{6,5},{7,8},{8,7},{9,10},{10,9},{11,... | collective-permute-start | bytes 614408 | tf_op jit(solution)/shard_map/ppermute | solution.py:479
  6.3 6.8 %collective-permute-start.1 = (bf16[800,128]{1,0:T(8,128)(2,1)S(1)}, bf16[800,128]{1,0:T(8,128)(2,1)S(1)}, u32[]{:S(2)}, u32[]{:S(2)}) collective-permute-start(bf16[800,128]{1,0:T(8,128)(2,1)S(1)} %get-tuple-element.27), channel_id=1, source_target_pairs={{0,1},{1,0},{2,3},{3,2},{4,5},{5,4},{6,7},{7,6},{8,9},{9,8},{10,11... | collective-permute-start | bytes 614408 | tf_op jit(solution)/shard_map/ppermute | solution.py:479
  11.2 0.7 copy-start.7
  11.2 0.7 copy-start.5
  11.2 0.7 copy-start.6
  11.9 0.7 %copy-start.4 = (f32[3,3,3,64]{3,2,1,0:T(4,128)S(1)}, f32[3,3,3,64]{3,2,1,0:T(4,128)}, u32[]{:S(2)}) copy-start(f32[3,3,3,64]{3,2,1,0:T(4,128)} %lpips_ref.1) | copy-start | bytes 20740
  12.6 0.9 %copy-start = (bf16[1,4,256,128]{3,2,1,0:T(8,128)(2,1)S(1)}, bf16[1,4,256,128]{3,2,1,0:T(8,128)(2,1)}, u32[]{:S(2)}) copy-start(bf16[1,4,256,128]{3,2,1,0:T(8,128)(2,1)} %param.8) | copy-start | bytes 786436
  12.6 1.0 %copy-start.1 = (f32[1,4,256,3]{2,1,3,0:T(4,128)S(1)}, f32[1,4,256,3]{2,1,3,0:T(4,128)}, u32[]{:S(2)}) copy-start(f32[1,4,256,3]{2,1,3,0:T(4,128)} %param.11) | copy-start | bytes 36868
  32.1 26.8 %all-to-all-start.1 = ((bf16[16,24,128]{2,1,0:T(8,128)(2,1)}), bf16[16,24,128]{2,1,0:T(8,128)(2,1)S(1)}, u32[]{:S(2)}, u32[]{:S(2)}) async-start(bf16[16,24,128]{2,1,0:T(8,128)(2,1)} %shard_map.114), calls=%async_computation.1 | async-start | bytes 196608 | tf_op jit(solution)/shard_map/all_to_all | solution.py:462
  47.0 5.9 %collective-permute-start.2 = (bf16[256,128]{1,0:T(8,128)(2,1)S(1)}, bf16[256,128]{1,0:T(8,128)(2,1)S(1)}, u32[]{:S(2)}, u32[]{:S(2)}) collective-permute-start(bf16[256,128]{1,0:T(8,128)(2,1)S(1)} %get-tuple-element.38), channel_id=1, source_target_pairs={{1,2},{2,1},{3,4},{4,3},{5,6},{6,5},{7,8},{8,7},{9,10},{10,9},{11,... | collective-permute-start | bytes 196616 | tf_op jit(solution)/shard_map/ppermute | solution.py:488
  49.6 3.3 %collective-permute-start.3 = (bf16[256,128]{1,0:T(8,128)(2,1)S(1)}, bf16[256,128]{1,0:T(8,128)(2,1)S(1)}, u32[]{:S(2)}, u32[]{:S(2)}) collective-permute-start(bf16[256,128]{1,0:T(8,128)(2,1)S(1)} %get-tuple-element.39), channel_id=1, source_target_pairs={{0,1},{1,0},{2,3},{3,2},{4,5},{5,4},{6,7},{7,6},{8,9},{9,8},{10,11... | collective-permute-start | bytes 196616 | tf_op jit(solution)/shard_map/ppermute | solution.py:488
where the time goes:
time: 70 us; the launch traced here: 69.5 us
  starting transfers between devices  28.8 us (41%)
  blocking collectives  24.3 us (35%)
  Pallas kernels  7.8 us (11%)
  waiting for transfers between devices  5.9 us (8%)
  local copies, waits for them, and re-layouts  1.86 us (3%)
  between operations  0.79 us (1%)
    all_to_all x2, blocking collectives, swap(): return lax.all_to_all(array, axes, split_axis=0, concat_axis=0, tiled=True)  24.3 us
    all_to_all x1, starting transfers between devices, swap(): return lax.all_to_all(array, axes, split_axis=0, concat_axis=0, tiled=True)  14.9 us
    ppermute x2, starting transfers between devices, body(): lax.ppermute(far, ROWS, off_chip)  7.08 us
    ppermute x2, starting transfers between devices, body(): lax.ppermute(near, ROWS, on_chip)  6.84 us
    all_to_all x1, waiting for transfers between devices, swap(): return lax.all_to_all(array, axes, split_axis=0, concat_axis=0, tiled=True)  4.53 us
    pallas_call x1, Pallas kernels, tile_step(): call(main_kernel, (shape(3, ROWS_LOC, COLS), shape(ROWS_LOC, COLS, CH, dt...  3.36 us
    unnamed x16, local copies, waits for them, and re-layouts  1.86 us
    pallas_call x1, Pallas kernels, back_step(): call(back_kernel, (shape(ROWS_LOC, COLS, CH, dtype=jnp.bfloat16), shape(3...  1.51 us
  transfers between devices with their start and end apart: 5, of which 2 were waited for; matrix products, arithmetic and copies ran while one was open for 0% of the time, Pallas kernels for 3%

commit v1 on v0

--- a/solution.py
+++ b/solution.py
@@ -281,7 +281,7 @@
                 while start < tap * 16 + 16:
                     part, inner = divmod(start, 18)
                     count = min(18 - inner, tap * 16 + 16 - start)
-                    at = ((d // 2) * 8 + part) * 2 * BLOCK + (d % 2) * BLOCK + inner
+                    at = (part * 4 + d // 2) * 2 * BLOCK + (d % 2) * BLOCK + inner
                     packed[pl.ds(at, count), :] = block[start - tap * 16 : start - tap * 16 + count]
                     start += count
     for d in range(8):
@@ -289,7 +289,7 @@
             line = grad_out[c : c + 1]
             if d:
                 line = pltpu.roll(line, CH - 16 * d, 1)
-            packed[pl.ds(((d // 2) * 8 + c) * 2 * BLOCK + (d % 2) * BLOCK + 18, 1), :] = line
+            packed[pl.ds((c * 4 + d // 2) * 2 * BLOCK + (d % 2) * BLOCK + 18, 1), :] = line
     piece_ref[...] = packed[...].astype(bf16)
 
 
@@ -481,7 +481,7 @@
         conv_weight, disc_weight, disc_head, lpips_weight, lpips_lin, out_weight
     )
     recon, grad_pre, near, far, pieces = tile_step(tile, far, own, truth, near, *tables)
-    pieces = swap(pieces.reshape(32, 2 * BLOCK, CH), ("y", "x", "core"))
+    pieces = swap(pieces.reshape(32, 2 * BLOCK, CH), ("x", "core", "y"))
     pieces = call(first_sum_kernel, shape(16, PADDED, CH, dtype=jnp.bfloat16))(pieces)
     pieces, near, far = lax.optimization_barrier((pieces, near, far))
     pieces = swap(pieces, ("zh", "zl"))

time: 70 us -> 70.2 us (level)
  transfers between devices with their start and end apart: 5 -> 5, of which waited for: 2 -> 3; matrix products, arithmetic and copies ran while one was open for 0% -> 0% of each run, Pallas kernels for 3% -> 3%
where the time goes in v1:
time: 70.2 us; the launch traced here: 69.7 us
  starting transfers between devices  29.1 us (41%)
  blocking collectives  24.6 us (35%)
  Pallas kernels  7.8 us (11%)
  waiting for transfers between devices  5.53 us (8%)
  local copies, waits for them, and re-layouts  1.86 us (3%)
  between operations  0.78 us (1%)
    all_to_all x2, blocking collectives, swap(): return lax.all_to_all(array, axes, split_axis=0, concat_axis=0, tiled=True)  24.6 us
    all_to_all x1, starting transfers between devices, swap(): return lax.all_to_all(array, axes, split_axis=0, concat_axis=0, tiled=True)  14.9 us
    ppermute x2, starting transfers between devices, body(): lax.ppermute(far, ROWS, off_chip)  7.38 us
    ppermute x2, starting transfers between devices, body(): lax.ppermute(near, ROWS, on_chip)  6.84 us
    all_to_all x1, waiting for transfers between devices, swap(): return lax.all_to_all(array, axes, split_axis=0, concat_axis=0, tiled=True)  4.31 us
    pallas_call x1, Pallas kernels, tile_step(): call(main_kernel, (shape(3, ROWS_LOC, COLS), shape(ROWS_LOC, COLS, CH, dt...  3.35 us
    unnamed x16, local copies, waits for them, and re-layouts  1.86 us
    pallas_call x1, Pallas kernels, back_step(): call(back_kernel, (shape(ROWS_LOC, COLS, CH, dtype=jnp.bfloat16), shape(3...  1.51 us
  transfers between devices with their start and end apart: 5, of which 3 were waited for; matrix products, arithmetic and copies ran while one was open for 0% of the time, Pallas kernels for 3%

profile of v1, /device:TPU:1, one launch (start us, length us, event | category | flops | bytes accessed | tf_op | source)
XLA Modules:
  0.0 69.7 jit_solution(8653905802062428192)
XLA Ops:
  0.6 0.0 copy-start.2
  0.6 0.0 copy-start.3
  0.7 1.1 %shard_map.111 = (bf16[800,128]{1,0:T(8,128)(2,1)S(1)}, bf16[800,128]{1,0:T(8,128)(2,1)S(1)}) custom-call(s32[1]{0:T(128)} %bitcast.tile_ref, bf16[1024,128]{1,0:T(8,128)(2,1)} %bitcast.18, f32[3,4,256]{2,1,0:T(4,128)} %bitcast.20), custom_call_target="tpu_custom_call" | custom-call | bytes 1048576 | tf_op jit(solution)/shard_map/pallas_call | solution.py:382
  1.8 4.5 %collective-permute-start = (bf16[800,128]{1,0:T(8,128)(2,1)S(1)}, bf16[800,128]{1,0:T(8,128)(2,1)S(1)}, u32[]{:S(2)}, u32[]{:S(2)}) collective-permute-start(bf16[800,128]{1,0:T(8,128)(2,1)S(1)} %get-tuple-element.26), channel_id=1, source_target_pairs={{1,2},{2,1},{3,4},{4,3},{5,6},{6,5},{7,8},{8,7},{9,10},{10,9},{11,... | collective-permute-start | bytes 614408 | tf_op jit(solution)/shard_map/ppermute | solution.py:479
  6.3 4.9 %collective-permute-start.1 = (bf16[800,128]{1,0:T(8,128)(2,1)S(1)}, bf16[800,128]{1,0:T(8,128)(2,1)S(1)}, u32[]{:S(2)}, u32[]{:S(2)}) collective-permute-start(bf16[800,128]{1,0:T(8,128)(2,1)S(1)} %get-tuple-element.27), channel_id=1, source_target_pairs={{0,1},{1,0},{2,3},{3,2},{4,5},{5,4},{6,7},{7,6},{8,9},{9,8},{10,11... | collective-permute-start | bytes 614408 | tf_op jit(solution)/shard_map/ppermute | solution.py:479
  11.2 0.0 copy-start.7
  11.2 0.0 copy-start.5
  11.2 0.0 copy-start.6
  11.2 0.0 copy-done.2
  11.3 0.0 copy-done.3
  11.3 0.6 copy-done.7
  11.9 0.0 copy-done.5
  11.9 0.0 copy-done.6
  11.9 0.0 copy-start.4
  11.9 0.7 %copy-done.4 = f32[3,3,3,64]{3,2,1,0:T(4,128)S(1)} copy-done((f32[3,3,3,64]{3,2,1,0:T(4,128)S(1)}, f32[3,3,3,64]{3,2,1,0:T(4,128)}, u32[]{:S(2)}) %copy-start.4) | copy-done | bytes 6936
  12.6 0.0 copy-start
  12.6 0.0 copy-start.1
  12.6 0.5 shard_map.112
  13.1 0.0 collective-permute-done.far_ref
  13.1 0.0 collective-permute-done.1.near_ref
  13.1 0.5 copy-done
  13.6 0.0 copy-done.1
  13.6 3.4 %shard_map.113 = (f32[3,4,256]{2,1,0:T(4,128)S(1)}, bf16[4,256,128]{2,1,0:T(8,128)(2,1)S(1)}, bf16[256,128]{1,0:T(8,128)(2,1)S(1)}, bf16[256,128]{1,0:T(8,128)(2,1)S(1)}, bf16[1280,128]{1,0:T(8,128)(2,1)S(1)}) custom-call(s32[1]{0:T(128)} %bitcast.tile_ref, bf16[800,128]{1,0:T(8,128)(2,1)S(1)} %collective-permute-done.far_ref, ...), custom_call_target="tpu_custom_call" | custom-call | flops 2147483648 | bytes 1048576 | tf_op jit(solution)/shard_map/pallas_call | solution.py:419
  16.9 14.4 %all_to_all.15.in_ref = bf16[32,40,128]{2,1,0:T(8,128)(2,1)S(1)} all-to-all(bf16[32,40,128]{2,1,0:T(8,128)(2,1)S(1)} %bitcast.17), channel_id=1, replica_groups=mesh['y'=4,'zh'=2,'zl'=8,'x'=4,'core'=2] {'x','core','y'}, dimensions={0} | all-to-all | bytes 655360 | tf_op jit(solution)/shard_map/all_to_all | solution.py:462
  31.3 0.7 %shard_map.114 = bf16[16,24,128]{2,1,0:T(8,128)(2,1)} custom-call(bf16[32,40,128]{2,1,0:T(8,128)(2,1)S(1)} %all_to_all.15.in_ref), custom_call_target="tpu_custom_call" | custom-call | bytes 1048576 | tf_op jit(solution)/shard_map/pallas_call | solution.py:485
  32.1 14.9 %all-to-all-start.1 = ((bf16[16,24,128]{2,1,0:T(8,128)(2,1)}), bf16[16,24,128]{2,1,0:T(8,128)(2,1)S(1)}, u32[]{:S(2)}, u32[]{:S(2)}) async-start(bf16[16,24,128]{2,1,0:T(8,128)(2,1)} %shard_map.114), calls=%async_computation.1 | async-start | bytes 196608 | tf_op jit(solution)/shard_map/all_to_all | solution.py:462
  47.0 2.9 %collective-permute-start.2 = (bf16[256,128]{1,0:T(8,128)(2,1)S(1)}, bf16[256,128]{1,0:T(8,128)(2,1)S(1)}, u32[]{:S(2)}, u32[]{:S(2)}) collective-permute-start(bf16[256,128]{1,0:T(8,128)(2,1)S(1)} %get-tuple-element.38), channel_id=1, source_target_pairs={{1,2},{2,1},{3,4},{4,3},{5,6},{6,5},{7,8},{8,7},{9,10},{10,9},{11,... | collective-permute-start | bytes 196616 | tf_op jit(solution)/shard_map/ppermute | solution.py:488
  49.9 1.9 %collective-permute-start.3 = (bf16[256,128]{1,0:T(8,128)(2,1)S(1)}, bf16[256,128]{1,0:T(8,128)(2,1)S(1)}, u32[]{:S(2)}, u32[]{:S(2)}) collective-permute-start(bf16[256,128]{1,0:T(8,128)(2,1)S(1)} %get-tuple-element.39), channel_id=1, source_target_pairs={{0,1},{1,0},{2,3},{3,2},{4,5},{5,4},{6,7},{7,6},{8,9},{9,8},{10,11... | collective-permute-start | bytes 196616 | tf_op jit(solution)/shard_map/ppermute | solution.py:488
  51.8 1.1 %collective-permute-done.2.far_ref = bf16[256,128]{1,0:T(8,128)(2,1)S(1)} collective-permute-done((bf16[256,128]{1,0:T(8,128)(2,1)S(1)}, bf16[256,128]{1,0:T(8,128)(2,1)S(1)}, u32[]{:S(2)}, u32[]{:S(2)}) %collective-permute-start.2) | collective-permute-done | bytes 65568 | tf_op jit(solution)/shard_map/ppermute | solution.py:488
  52.9 0.2 collective-permute-done.3.near_ref
  53.0 1.5 %shard_map.115 = (bf16[4,256,128]{2,1,0:T(8,128)(2,1)}, f32[3,4,256]{2,1,0:T(4,128)}) custom-call(s32[1]{0:T(128)} %bitcast.tile_ref, bf16[4,256,128]{2,1,0:T(8,128)(2,1)S(1)} %get-tuple-element.37.grad_ref, bf16[256,128]{1,0:T(8,128)(2,1)S(1)} %collective-permute-done.2.far_ref, bf16[256,128]{1,0:T(8,128)(2,1)S(1)} %collective-permute-done.3.near_ref, ...), custom_call_target="tpu_custom_call" | custom-call | flops 1073741824 | bytes 1048576 | tf_op jit(solution)/shard_map/pallas_call | solution.py:449
  54.5 4.3 %all-to-all-done.1.in_ref = bf16[16,24,128]{2,1,0:T(8,128)(2,1)S(1)} async-done(((bf16[16,24,128]{2,1,0:T(8,128)(2,1)}), bf16[16,24,128]{2,1,0:T(8,128)(2,1)S(1)}, u32[]{:S(2)}, u32[]{:S(2)}) %all-to-all-start.1) | async-done | bytes 98336 | tf_op jit(solution)/shard_map/all_to_all | solution.py:462
  58.9 10.2 %all_to_all.16.in_ref = f32[8,24,128]{2,1,0:T(8,128)S(1)} all-to-all(f32[8,24,128]{2,1,0:T(8,128)S(1)} %shard_map.116), channel_id=1, replica_groups=mesh['y'=4,'zh'=2,'zl'=8,'x'=4,'core'=2] {'x','core'}, dimensions={0} | all-to-all | bytes 196608 | tf_op jit(solution)/shard_map/all_to_all | solution.py:462
  69.1 0.6 shard_map.117
  (1 shorter events, 0.0 us)
Async XLA Ops:
  0.6 10.6 %copy-start.2 = (bf16[3,3,128,128]{3,2,1,0:T(8,128)(2,1)S(1)}, bf16[3,3,128,128]{3,2,1,0:T(8,128)(2,1)}, u32[]{:S(2)}) copy-start(bf16[3,3,128,128]{3,2,1,0:T(8,128)(2,1)} %conv_ref.3) | copy-start | bytes 884740
  0.6 10.6 %copy-start.3 = (f32[3,3,3,64]{3,2,1,0:T(4,128)S(1)}, f32[3,3,3,64]{3,2,1,0:T(4,128)}, u32[]{:S(2)}) copy-start(f32[3,3,3,64]{3,2,1,0:T(4,128)} %disc_ref.1) | copy-start | bytes 20740
  1.8 11.3 %collective-permute-start = (bf16[800,128]{1,0:T(8,128)(2,1)S(1)}, bf16[800,128]{1,0:T(8,128)(2,1)S(1)}, u32[]{:S(2)}, u32[]{:S(2)}) collective-permute-start(bf16[800,128]{1,0:T(8,128)(2,1)S(1)} %get-tuple-element.26), channel_id=1, source_target_pairs={{1,2},{2,1},{3,4},{4,3},{5,6},{6,5},{7,8},{8,7},{9,10},{10,9},{11,... | collective-permute-start | bytes 614408 | tf_op jit(solution)/shard_map/ppermute | solution.py:479
  6.3 6.8 %collective-permute-start.1 = (bf16[800,128]{1,0:T(8,128)(2,1)S(1)}, bf16[800,128]{1,0:T(8,128)(2,1)S(1)}, u32[]{:S(2)}, u32[]{:S(2)}) collective-permute-start(bf16[800,128]{1,0:T(8,128)(2,1)S(1)} %get-tuple-element.27), channel_id=1, source_target_pairs={{0,1},{1,0},{2,3},{3,2},{4,5},{5,4},{6,7},{7,6},{8,9},{9,8},{10,11... | collective-permute-start | bytes 614408 | tf_op jit(solution)/shard_map/ppermute | solution.py:479
  11.2 0.7 copy-start.7
  11.2 0.7 copy-start.5
  11.2 0.7 copy-start.6
  11.9 0.7 %copy-start.4 = (f32[3,3,3,64]{3,2,1,0:T(4,128)S(1)}, f32[3,3,3,64]{3,2,1,0:T(4,128)}, u32[]{:S(2)}) copy-start(f32[3,3,3,64]{3,2,1,0:T(4,128)} %lpips_ref.1) | copy-start | bytes 20740
  12.6 0.9 %copy-start = (bf16[1,4,256,128]{3,2,1,0:T(8,128)(2,1)S(1)}, bf16[1,4,256,128]{3,2,1,0:T(8,128)(2,1)}, u32[]{:S(2)}) copy-start(bf16[1,4,256,128]{3,2,1,0:T(8,128)(2,1)} %param.8) | copy-start | bytes 786436
  12.6 1.0 %copy-start.1 = (f32[1,4,256,3]{2,1,3,0:T(4,128)S(1)}, f32[1,4,256,3]{2,1,3,0:T(4,128)}, u32[]{:S(2)}) copy-start(f32[1,4,256,3]{2,1,3,0:T(4,128)} %param.11) | copy-start | bytes 36868
  32.1 26.8 %all-to-all-start.1 = ((bf16[16,24,128]{2,1,0:T(8,128)(2,1)}), bf16[16,24,128]{2,1,0:T(8,128)(2,1)S(1)}, u32[]{:S(2)}, u32[]{:S(2)}) async-start(bf16[16,24,128]{2,1,0:T(8,128)(2,1)} %shard_map.114), calls=%async_computation.1 | async-start | bytes 196608 | tf_op jit(solution)/shard_map/all_to_all | solution.py:462
  47.0 5.9 %collective-permute-start.2 = (bf16[256,128]{1,0:T(8,128)(2,1)S(1)}, bf16[256,128]{1,0:T(8,128)(2,1)S(1)}, u32[]{:S(2)}, u32[]{:S(2)}) collective-permute-start(bf16[256,128]{1,0:T(8,128)(2,1)S(1)} %get-tuple-element.38), channel_id=1, source_target_pairs={{1,2},{2,1},{3,4},{4,3},{5,6},{6,5},{7,8},{8,7},{9,10},{10,9},{11,... | collective-permute-start | bytes 196616 | tf_op jit(solution)/shard_map/ppermute | solution.py:488
  49.9 3.1 %collective-permute-start.3 = (bf16[256,128]{1,0:T(8,128)(2,1)S(1)}, bf16[256,128]{1,0:T(8,128)(2,1)S(1)}, u32[]{:S(2)}, u32[]{:S(2)}) collective-permute-start(bf16[256,128]{1,0:T(8,128)(2,1)S(1)} %get-tuple-element.39), channel_id=1, source_target_pairs={{0,1},{1,0},{2,3},{3,2},{4,5},{5,4},{6,7},{7,6},{8,9},{9,8},{10,11... | collective-permute-start | bytes 196616 | tf_op jit(solution)/shard_map/ppermute | solution.py:488
